TPU v7x, 256 devices: a whole 4x4x8 slice. The times are simulated.
256 devices in a mesh: dec: 16 (over z, core), tp: 16 (over y, x).
Axes of the slice: x: 4, y: 4, z: 8, core: 2. Of those that a mesh axis runs over, the one named last changes fastest.
Arguments:
- hidden: float32 [16, 32, 4, 4096], P('dec', 'tp'), may hold values from -500 to 500
- norm_gain: float32 [4096], replicated, may hold values from 0.5 to 1.5
- lm_head: bfloat16 [131072, 4096], P(('dec', 'tp')), may hold values from -1 to 1
- token_ids: int32 [16, 32, 4], P('dec'), may hold values from 0 to 131071
- doc_counts: int32 [16], P('dec'), may hold values from 8 to 32, as said below
Outputs:
- hyp_score: float32 [16, 32], P('dec', 'tp')
- posterior: float32 [16, 32], P('dec', 'tp')
Inputs may be any that keep to these rules, and one draw needn't show every extreme that they name: Document d's live hypotheses are its slots 0 to doc_counts[d] - 1; some document has 32.
All inputs are finite; a program needn't handle non-finite values.
Results may differ from a plain program's by a relative error of at most 0.0021.
Values may be sent and summed in bfloat16 or wider, within the bound.
No kernel may reach another device: no remote copies, remote signals or barrier semaphores. Data moves between devices by JAX's collectives and lax.ppermute only.
A program may use at most 64 MiB of HBM per device.

v0:
```python
import jax
import jax.numpy as jnp
from jax import lax
from jax.sharding import PartitionSpec as P


def rms_normed(hidden, norm_gain):
    flat = hidden.reshape(-1, hidden.shape[-1])
    meansq = jnp.mean(flat * flat, axis=1, keepdims=True)
    return (flat * lax.rsqrt(meansq + 1e-05) * norm_gain).astype(jnp.bfloat16)


def body(hidden, norm_gain, lm_head, token_ids, doc_counts):
    tp_count = lax.axis_size("tp")
    tp_index = lax.axis_index("tp")
    dec_index = lax.axis_index("dec")
    slot_count = hidden.shape[1]
    length = hidden.shape[2]
    vocab_rows = lm_head.shape[0]
    normed = rms_normed(hidden, norm_gain)
    doc_ids = token_ids[0]
    vocab_start = (dec_index * tp_count + tp_index) * vocab_rows
    own_slots = tp_index * slot_count + jnp.arange(slot_count, dtype=jnp.int32)
    sent_ids = lax.dynamic_slice_in_dim(doc_ids, tp_index * slot_count, slot_count, 0).reshape(-1)
    seg_rows = lax.all_gather(normed, ("dec", "tp"), axis=0, tiled=True)
    seg_ids = lax.all_gather(sent_ids, ("dec", "tp"), axis=0, tiled=True)
    logits = lax.dot_general(
        seg_rows, lm_head, (((1,), (1,)), ((), ())), preferred_element_type=jnp.float32
    )
    peak_value = jnp.max(logits, axis=1)
    exp_total = jnp.sum(jnp.exp(logits - peak_value[:, None]), axis=1)
    local_ids = seg_ids - vocab_start
    matches = jnp.arange(vocab_rows, dtype=jnp.int32)[None, :] == local_ids[:, None]
    target = jnp.sum(jnp.where(matches, logits, 0.0), axis=1)
    fresh = (peak_value, exp_total, target)
    peak_value, exp_total, target = tuple((new for new in fresh))
    block_slot = jnp.arange(tp_count * slot_count, dtype=jnp.int32)
    block_rows = tp_count * slot_count * length
    global_peak = lax.pmax(peak_value, ("dec", "tp"))
    scaled = exp_total * jnp.exp(peak_value - global_peak)
    sum_exp, target_sum = lax.psum((scaled, target), ("dec", "tp"))
    token_logp = target_sum - (global_peak + jnp.log(sum_exp))
    doc_logp = lax.dynamic_slice_in_dim(token_logp, dec_index * block_rows, block_rows, 0)
    block_scores = jnp.sum(doc_logp.reshape(-1, length), axis=1) / length
    alive = block_slot < doc_counts[0]
    best_score = jnp.max(jnp.where(alive, block_scores, -jnp.inf))
    doc_norm = best_score + jnp.log(
        jnp.sum(jnp.exp(jnp.where(alive, block_scores - best_score, -jnp.inf)))
    )
    picked = jnp.take(block_scores, own_slots)
    own_alive = own_slots < doc_counts[0]
    hyp_score = jnp.where(own_alive, picked, 0.0)[None, :]
    posterior = jnp.where(own_alive, picked - doc_norm, 0.0)[None, :]
    return (hyp_score, posterior)


def solution(mesh):
    placed = (
        P("dec", "tp", None, None),
        P(),
        P(("dec", "tp"), None),
        P("dec", None, None),
        P("dec"),
    )
    return jax.shard_map(
        body,
        mesh=mesh,
        in_specs=placed,
        out_specs=(P("dec", "tp"), P("dec", "tp")),
        check_vma=False,
    )
```

profile of v0, /device:TPU:2, one launch (start us, length us, event | category | flops | bytes accessed | tf_op | source)
XLA Modules:
  0.0 318.0 jit_solution(200541689986261581)
XLA Ops:
  7.2 0.0 copy-start
  7.2 0.0 all-gather.2.cloned.1.call-start
  7.2 1.0 reshape.106
  8.2 1.0 multiply_reduce_fusion
  9.2 0.1 rsqrt.12
  9.3 1.4 multiply_convert_fusion
  10.7 0.0 all-gather.2.cloned.1.call-update
  11.4 0.0 copy-done
  11.4 0.1 constant_dynamic-slice_fusion
  11.5 0.1 copy.8
  11.6 0.1 reshape.116
  11.7 0.2 dynamic-update-slice
  11.9 79.2 %all-reduce = s32[2048]{0:T(1024)S(1)} all-reduce(s32[2048]{0:T(1024)S(1)} %dynamic-update-slice), channel_id=1, replica_groups=mesh['dec'=16,'tp'=16] {'dec','tp'}, use_global_device_ids=true, to_apply=%add | all-reduce | flops 2048 | bytes 16384
  91.1 48.8 %all-gather.2.cloned.1.call-done = bf16[2048,4096]{1,0:T(8,128)(2,1)} async-done(((bf16[8,4096]{1,0:T(8,128)(2,1)}), bf16[2048,4096]{1,0:T(8,128)(2,1)}) %all-gather.2.cloned.1.call-update) | async-done | bytes 16777232 | tf_op jit(solution)/shard_map/all_gather | solution.py:25
  140.0 15.0 %fusion.4 = (f32[2048]{0:T(1024)S(1)}, f32[2048,512]{0,1:T(8,128)}) fusion(bf16[2048,4096]{1,0:T(8,128)(2,1)} %all-gather.2.cloned.1.call-done, bf16[512,4096]{1,0:T(8,128)(2,1)} %param.7), kind=kOutput, calls=%fused_computation.27 | convolution fusion | flops 8590981120 | bytes 25174016 | tf_op jit(solution)/shard_map/dot_general | solution.py:27
  155.0 74.4 %pmax.7 = f32[2048]{0:T(1024)S(1)} all-reduce(f32[2048]{0:T(1024)S(1)} %get-tuple-element.10), channel_id=1, replica_groups=mesh['dec'=16,'tp'=16] {'dec','tp'}, use_global_device_ids=true, to_apply=%region_4.5 | all-reduce | flops 2048 | bytes 16384 | tf_op jit(solution)/shard_map/pmax | solution.py:39
  229.4 3.3 %exponential_reduce_fusion = (f32[2048]{0:T(1024)S(1)}, f32[2048]{0:T(1024)S(1)}) fusion(f32[2048,512]{0,1:T(8,128)} %get-tuple-element.11, f32[2048]{0:T(1024)S(1)} %get-tuple-element.10, s32[2048]{0:T(1024)S(1)} %broadcast_subtract_fusion), kind=kLoop, calls=%fused_computation.1 | loop fusion | flops 5238784 | bytes 4227072 | tf_op jit(solution)/shard_map/reduce_sum | solution.py:31
  232.7 73.7 %all-reduce.1 = (f32[2048]{0:T(1024)S(1)}, f32[2048]{0:T(1024)S(1)}) all-reduce(f32[2048]{0:T(1024)S(1)} %get-tuple-element.3, f32[2048]{0:T(1024)S(1)} %exponential_multiply_fusion), channel_id=1, replica_groups=mesh['dec'=16,'tp'=16] {'dec','tp'}, use_global_device_ids=true, to_apply=%region_2.0 | all-reduce | flops 4096 | bytes 32768 | tf_op jit(solution)/shard_map/psum | solution.py:41
  306.4 0.1 dynamic-slice_subtract_fusion
  306.5 0.1 reshape.107
  306.6 0.1 reduce_sum.48
  306.7 0.6 fusion
  307.3 1.3 fusion.2
  309.9 0.6 gather_fusion
  310.6 0.5 compare_select_fusion.4
  (6 shorter events, 0.0 us)
Async XLA Ops:
  7.2 4.2 %copy-start = (s32[1,32,4]{1,2,0:T(4,128)S(1)}, s32[1,32,4]{1,2,0:T(4,128)}, u32[]{:S(2)}) copy-start(s32[1,32,4]{1,2,0:T(4,128)} %param.8) | copy-start | bytes 1540
  7.2 132.8 %all-gather.2.cloned.1.call-start = ((), (), s32[]{:S(2)}) async-start(), calls=%async_computation | async-start | bytes 16842752 | tf_op jit(solution)/shard_map/all_gather | solution.py:25
Sparse Core Ops, SparseCore 0:
  11.7 128.2 all-gather.1
where the time goes:
time: 320 us; the launch traced here: 318 us
  blocking collectives  227 us (71%)
  waiting for transfers between devices  48.8 us (15%)
  between operations  16.1 us (5%)
  matrix products  15 us (5%)
  other arithmetic  8.36 us (3%)
    unnamed x1, blocking collectives  79.2 us
    pmax x1, blocking collectives, body(): global_peak = lax.pmax(peak_value, ('dec', 'tp'))  74.4 us
    psum x1, blocking collectives, body(): sum_exp, target_sum = lax.psum((scaled, target), ('dec', 'tp'))  73.7 us
    all_gather x1, waiting for transfers between devices, body(): seg_rows = lax.all_gather(normed, ('dec', 'tp'), axis=0, tiled=True)  48.8 us
    dot_general x1, matrix products, body(): lax.dot_general(seg_rows, lm_head, (((1,), (1,)), ((), ())), preferred_el...  15 us
  transfers between devices with their start and end apart: 1, of which 1 were waited for; matrix products, arithmetic and copies ran while one was open for 0% of the time, Pallas kernels for 0%

commit v1 on v0

v1 whole, which is shorter than its diff:
```python
import jax
import jax.numpy as jnp
from jax import lax
from jax.sharding import Mesh, PartitionSpec as P


def rms_normed(hidden, norm_gain):
    flat = hidden.reshape(-1, hidden.shape[-1])
    meansq = jnp.mean(flat * flat, axis=1, keepdims=True)
    return (flat * lax.rsqrt(meansq + 1e-05) * norm_gain).astype(jnp.bfloat16)


def spread(block, axis):
    count = lax.axis_size(axis)
    return lax.all_to_all(
        jnp.broadcast_to(block[None], (count,) + block.shape), axis, 0, 0, tiled=True
    )


def shifted(block, axis, step):
    count = lax.axis_size(axis)
    return lax.ppermute(block, axis, [(i, (i + step) % count) for i in range(count)])


def joined(parts, axis):
    count = len(parts)
    index = lax.axis_index(axis)
    stacked = jnp.stack(parts[::-1])
    return jnp.roll(stacked, index + 1, axis=0)


def merge_logs(logs):
    peak = jnp.max(logs, axis=0)
    return peak + jnp.log(jnp.sum(jnp.exp(logs - peak[None]), axis=0))


def body(hidden, norm_gain, lm_head, token_ids, doc_counts):
    z, c, y, x = (lax.axis_index(a) for a in "zcyx")
    nz, nc, ny, nx = (lax.axis_size(a) for a in "zcyx")
    tp_count = ny * nx
    tp_index = y * nx + x
    slots, length = hidden.shape[1], hidden.shape[2]
    rows = slots * length
    vocab_rows, width = lm_head.shape
    tokens = tp_count * rows

    other_head = shifted(lm_head, "c", 1)
    normed = rms_normed(hidden, norm_gain)
    ids = token_ids.reshape(-1)
    digits = jnp.stack([ids // 65536, (ids // 256) % 256, ids % 256])
    digits = jnp.pad(digits, ((0, rows - 3), (0, 0))).astype(jnp.bfloat16)
    planes = spread(jnp.concatenate([normed, digits], axis=1), "z")
    got = planes[:, :3, width:].astype(jnp.int32)
    all_ids = got[:, 0] * 65536 + got[:, 1] * 256 + got[:, 2]

    half = nz // 2
    block_a = spread(planes[:half, :, :width], "y")
    block_b = spread(planes[half:, :, :width], "x")
    parts_a = [block_a] + [shifted(block_a, "x", k) for k in range(1, nx)]
    parts_b = [block_b] + [shifted(block_b, "y", k) for k in range(1, ny)]

    heads = (lm_head, other_head)
    starts = [((z * nc + core) * tp_count + tp_index) * vocab_rows for core in (c, nc - 1 - c)]
    ids_grid = all_ids.reshape(nz, ny, nx, rows)
    vocab = jnp.arange(vocab_rows, dtype=jnp.int32)

    def stats(block, block_ids):
        flat = block.reshape(-1, width)
        flat_ids = block_ids.reshape(-1)
        logits = [
            lax.dot_general(flat, head, (((1,), (1,)), ((), ())), preferred_element_type=jnp.float32)
            for head in heads
        ]
        peak = jnp.maximum(jnp.max(logits[0], axis=1), jnp.max(logits[1], axis=1))
        total = sum(jnp.sum(jnp.exp(part - peak[:, None]), axis=1) for part in logits)
        target = sum(
            jnp.sum(jnp.where(vocab[None, :] == (flat_ids - start)[:, None], part, 0.0), axis=1)
            for part, start in zip(logits, starts)
        )
        return jnp.stack([peak + jnp.log(total), target])

    def pick(grid, axis, index, step, count):
        return jnp.take(grid, (index - step + count) % count, axis=axis)

    out_a = [
        stats(part, pick(ids_grid[:half], 2, x, k, nx).transpose(1, 0, 2))
        for k, part in enumerate(parts_a)
    ]
    out_b = [
        stats(part, pick(ids_grid[half:], 1, y, k, ny).transpose(1, 0, 2))
        for k, part in enumerate(parts_b)
    ]
    stats_a = joined(out_a, "x").reshape(nx, 2, ny, half, rows).transpose(3, 1, 2, 0, 4)
    stats_b = joined(out_b, "y").reshape(ny, 2, nx, half, rows).transpose(3, 1, 0, 2, 4)
    sent = jnp.concatenate([stats_a, stats_b]).reshape(nz, 2, tokens)
    mine = lax.all_to_all(sent, "z", 0, 0, tiled=True)
    partial = jnp.stack([merge_logs(mine[:, 0]), jnp.sum(mine[:, 1], axis=0)])
    whole = spread(partial, ("y", "x"))
    token_logp = jnp.sum(whole[:, 1], axis=0) - merge_logs(whole[:, 0])
    scores = jnp.sum(token_logp.reshape(-1, length), axis=1) / length
    alive = jnp.arange(scores.shape[0], dtype=jnp.int32) < doc_counts[0]
    best = jnp.max(jnp.where(alive, scores, -jnp.inf))
    doc_norm = best + jnp.log(jnp.sum(jnp.exp(jnp.where(alive, scores - best, -jnp.inf))))
    hyp_score = jnp.where(alive, scores, 0.0)
    posterior = jnp.where(alive, scores - doc_norm, 0.0)
    own = tp_index * slots
    return tuple(lax.dynamic_slice_in_dim(v, own, slots)[None, :] for v in (hyp_score, posterior))


def solution(mesh):
    cores = 2
    side = 4
    dec, tp = mesh.devices.shape
    fine = Mesh(mesh.devices.reshape(dec // cores, cores, tp // side, side), ("z", "c", "y", "x"))
    docs, slots = ("z", "c"), ("y", "x")
    return jax.shard_map(
        body,
        mesh=fine,
        in_specs=(
            P(docs, slots, None, None),
            P(),
            P(("z", "c", "y", "x"), None),
            P(docs, None, None),
            P(docs),
        ),
        out_specs=(P(docs, slots), P(docs, slots)),
        check_vma=False,
    )
```

time: 320 us -> 211 us (0.66)
  blocking collectives: 227 us -> 41.2 us
  matrix products: 15 us -> 51.1 us
  starting transfers between devices: 0.04 us -> 32.8 us
  waiting for transfers between devices: 48.8 us -> 66.9 us
  between operations: 16.1 us -> 3.32 us
  local copies, waits for them, and re-layouts: 2.24 us -> 8.33 us
    unnamed x1 -> x0, blocking collectives: 79.2 us -> none
    pmax x1 -> x0, blocking collectives: 74.4 us -> none  [body(): global_peak = lax.pmax(peak_value, ('dec', 'tp'))]
    psum x1 -> x0, blocking collectives: 73.7 us -> none  [body(): sum_exp, target_sum = lax.psum((scaled, target), ('dec', 'tp'))]
    all_gather x1 -> x0, waiting for transfers between devices: 48.8 us -> none  [body(): seg_rows = lax.all_gather(normed, ('dec', 'tp'), axis=0, tiled=True)]
    all_to_all x0 -> x3, waiting for transfers between devices: none -> 46 us  [spread(): lax.all_to_all(jnp.broadcast_to(block[None], (count,) + block.shape), axi...]
    all_to_all x0 -> x2, blocking collectives: none -> 41.2 us  [the longest x1 26.1 us: spread(): lax.all_to_all(jnp.broadcast_to(block[None], (count,) + block.shape), axi...]
    dot_general x1 -> x16, matrix products: 15 us -> 51.1 us  [stats(): lax.dot_general(flat, head, (((1,), (1,)), ((), ())), preferred_element_t...]
    all_to_all x0 -> x3, starting transfers between devices: none -> 24.5 us  [spread(): lax.all_to_all(jnp.broadcast_to(block[None], (count,) + block.shape), axi...]
  transfers between devices with their start and end apart: 1 -> 10, of which waited for: 1 -> 6; matrix products, arithmetic and copies ran while one was open for 0% -> 11% of each run, Pallas kernels for 0% -> 0%
where the time goes in v1:
time: 211 us
  waiting for transfers between devices  66.9 us (32%)
  matrix products  51.1 us (24%)
  blocking collectives  41.2 us (20%)
  starting transfers between devices  32.8 us (16%)
  local copies, waits for them, and re-layouts  8.33 us (4%)
  other arithmetic  6.89 us (3%)
  between operations  3.32 us (2%)
    dot_general x16, matrix products, stats(): lax.dot_general(flat, head, (((1,), (1,)), ((), ())), preferred_element_t...  51.1 us
    all_to_all x3, waiting for transfers between devices, spread(): lax.all_to_all(jnp.broadcast_to(block[None], (count,) + block.shape), axi...  46 us
    all_to_all x1, blocking collectives, spread(): lax.all_to_all(jnp.broadcast_to(block[None], (count,) + block.shape), axi...  26.1 us
    all_to_all x3, starting transfers between devices, spread(): lax.all_to_all(jnp.broadcast_to(block[None], (count,) + block.shape), axi...  24.5 us
    ppermute x7, waiting for transfers between devices, shifted(): lax.ppermute(block, axis, [(i, (i + step) % count) for i in range(count)])  20.9 us
    all_to_all x1, blocking collectives, body(): mine = lax.all_to_all(sent, 'z', 0, 0, tiled=True)  15.1 us
    ppermute x7, starting transfers between devices, shifted(): lax.ppermute(block, axis, [(i, (i + step) % count) for i in range(count)])  8.24 us
  transfers between devices with their start and end apart: 10, of which 6 were waited for; matrix products, arithmetic and copies ran while one was open for 11% of the time, Pallas kernels for 0%

profile of v1, /device:TPU:2, one launch (start us, length us, event | category | flops | bytes accessed | tf_op | source)
XLA Modules:
  0.0 210.6 jit_solution(12676024217720083638)
XLA Ops:
  4.5 26.1 %all_to_all.25 = bf16[8,8,4224]{2,1,0:T(8,128)(2,1)S(1)} all-to-all(bf16[8,8,4224]{2,1,0:T(8,128)(2,1)S(1)} %broadcast_in_dim.57), channel_id=1, replica_groups=mesh['z'=8,'c'=2,'y'=4,'x'=4] {'z'}, dimensions={0} | all-to-all | bytes 1081344 | tf_op jit(solution)/shard_map/all_to_all | solution.py:15
  31.7 4.5 %all-to-all-start.1 = ((bf16[4,4,8,4096]{3,2,1,0:T(8,128)(2,1)}), bf16[4,4,8,4096]{3,2,1,0:T(8,128)(2,1)S(1)}, u32[]{:S(2)}, u32[]{:S(2)}) async-start(bf16[4,4,8,4096]{3,2,1,0:T(8,128)(2,1)} %broadcast_in_dim.58), calls=%async_computation.1 | async-start | bytes 2097152 | tf_op jit(solution)/shard_map/all_to_all | solution.py:15
  36.4 13.0 %all-to-all-done.1 = bf16[4,4,8,4096]{3,2,1,0:T(8,128)(2,1)S(1)} async-done(((bf16[4,4,8,4096]{3,2,1,0:T(8,128)(2,1)}), bf16[4,4,8,4096]{3,2,1,0:T(8,128)(2,1)S(1)}, u32[]{:S(2)}, u32[]{:S(2)}) %all-to-all-start.1) | async-done | bytes 1048608 | tf_op jit(solution)/shard_map/all_to_all | solution.py:15
  49.5 1.1 broadcast_in_dim.60
  50.6 4.8 %all-to-all-start.2 = ((bf16[4,4,8,4096]{3,2,1,0:T(8,128)(2,1)}), bf16[4,4,8,4096]{3,2,1,0:T(8,128)(2,1)S(1)}, u32[]{:S(2)}, u32[]{:S(2)}) async-start(bf16[4,4,8,4096]{3,2,1,0:T(8,128)(2,1)} %broadcast_in_dim.60), calls=%async_computation.2 | async-start | bytes 2097152 | tf_op jit(solution)/shard_map/all_to_all | solution.py:15
  55.5 1.5 collective-permute-start.3
  59.4 2.6 %collective-permute-start = (bf16[4,4,8,4096]{3,2,1,0:T(8,128)(2,1)S(1)}, bf16[4,4,8,4096]{3,2,1,0:T(8,128)(2,1)}, u32[]{:S(2)}, u32[]{:S(2)}) collective-permute-start(bf16[4,4,8,4096]{3,2,1,0:T(8,128)(2,1)S(1)} %all-to-all-done.1), channel_id=1, source_target_pairs={{0,3},{1,0},{2,1},{3,2},{4,7},{5,4},{6,5},{7,6},{8,11},{9,8},{10,9... | collective-permute-start | bytes 3145736 | tf_op jit(solution)/shard_map/ppermute | solution.py:22
  62.0 27.4 %all-to-all-done.2 = bf16[4,4,8,4096]{3,2,1,0:T(8,128)(2,1)S(1)} async-done(((bf16[4,4,8,4096]{3,2,1,0:T(8,128)(2,1)}), bf16[4,4,8,4096]{3,2,1,0:T(8,128)(2,1)S(1)}, u32[]{:S(2)}, u32[]{:S(2)}) %all-to-all-start.2) | async-done | bytes 1048608 | tf_op jit(solution)/shard_map/all_to_all | solution.py:15
  90.0 4.1 %fusion.49 = (f32[128]{0:T(128)S(1)}, f32[128,512]{1,0:T(8,128)S(1)}) fusion(bf16[128,4096]{1,0:T(8,128)(2,1)S(1)} %bitcast.171, bf16[512,4096]{1,0:T(8,128)(2,1)} %param.13), kind=kOutput, calls=%fused_computation.200 | convolution fusion | flops 536936320 | bytes 5505536 | tf_op jit(solution)/shard_map/dot_general | solution.py:71
  94.1 2.2 %fusion.41 = (f32[128]{0:T(128)S(1)}, f32[128,512]{1,0:T(8,128)}) fusion(bf16[128,4096]{1,0:T(8,128)(2,1)S(1)} %bitcast.173, bf16[512,4096]{1,0:T(8,128)(2,1)S(1)} %copy-done), kind=kOutput, calls=%fused_computation.192 | convolution fusion | flops 536936320 | bytes 5505536 | tf_op jit(solution)/shard_map/dot_general | solution.py:71
  96.3 1.8 collective-permute-start.5
  98.1 1.6 fusion.47
  100.8 2.8 %fusion.45 = (f32[128]{0:T(128)S(1)}, f32[128,512]{1,0:T(8,128)S(1)}) fusion(bf16[128,4096]{1,0:T(8,128)(2,1)} %bitcast.8, bf16[512,4096]{1,0:T(8,128)(2,1)S(1)} %copy-done), kind=kOutput, calls=%fused_computation.196 | convolution fusion | flops 536936320 | bytes 5505536 | tf_op jit(solution)/shard_map/dot_general | solution.py:71
  103.6 7.3 %collective-permute-done = bf16[4,4,8,4096]{3,2,1,0:T(8,128)(2,1)} collective-permute-done((bf16[4,4,8,4096]{3,2,1,0:T(8,128)(2,1)S(1)}, bf16[4,4,8,4096]{3,2,1,0:T(8,128)(2,1)}, u32[]{:S(2)}, u32[]{:S(2)}) %collective-permute-start) | collective-permute-done | bytes 1048608 | tf_op jit(solution)/shard_map/ppermute | solution.py:22
  110.9 2.8 %fusion.43 = (f32[128]{0:T(128)S(1)}, f32[128,512]{1,0:T(8,128)S(1)}) fusion(bf16[128,4096]{1,0:T(8,128)(2,1)} %bitcast.1, bf16[512,4096]{1,0:T(8,128)(2,1)S(1)} %copy-done), kind=kOutput, calls=%fused_computation.194 | convolution fusion | flops 536936320 | bytes 5505536 | tf_op jit(solution)/shard_map/dot_general | solution.py:71
  113.7 8.6 %collective-permute-done.6 = bf16[4,4,8,4096]{3,2,1,0:T(8,128)(2,1)S(1)} collective-permute-done((bf16[4,4,8,4096]{3,2,1,0:T(8,128)(2,1)S(1)}, bf16[4,4,8,4096]{3,2,1,0:T(8,128)(2,1)S(1)}, u32[]{:S(2)}, u32[]{:S(2)}) %collective-permute-start.6) | collective-permute-done | bytes 1048608 | tf_op jit(solution)/shard_map/ppermute | solution.py:22
  122.4 2.2 %fusion.39 = (f32[128]{0:T(128)S(1)}, f32[128,512]{1,0:T(8,128)}) fusion(bf16[128,4096]{1,0:T(8,128)(2,1)S(1)} %bitcast.179, bf16[512,4096]{1,0:T(8,128)(2,1)S(1)} %copy-done), kind=kOutput, calls=%fused_computation.190 | convolution fusion | flops 536936320 | bytes 5505536 | tf_op jit(solution)/shard_map/dot_general | solution.py:71
  124.6 2.3 %fusion.37 = (f32[128]{0:T(128)S(1)}, f32[128,512]{1,0:T(8,128)}) fusion(bf16[128,4096]{1,0:T(8,128)(2,1)S(1)} %bitcast.177, bf16[512,4096]{1,0:T(8,128)(2,1)S(1)} %copy-done), kind=kOutput, calls=%fused_computation.188 | convolution fusion | flops 536936320 | bytes 5505536 | tf_op jit(solution)/shard_map/dot_general | solution.py:71
  126.9 5.0 %collective-permute-done.4 = bf16[4,4,8,4096]{3,2,1,0:T(8,128)(2,1)S(1)} collective-permute-done((bf16[4,4,8,4096]{3,2,1,0:T(8,128)(2,1)S(1)}, bf16[4,4,8,4096]{3,2,1,0:T(8,128)(2,1)S(1)}, u32[]{:S(2)}, u32[]{:S(2)}) %collective-permute-start.4) | collective-permute-done | bytes 1048608 | tf_op jit(solution)/shard_map/ppermute | solution.py:22
  131.9 1.6 fusion.35
  133.5 3.9 %fusion.50 = (f32[128]{0:T(128)S(1)}, f32[128,512]{1,0:T(8,128)S(1)}) fusion(bf16[128,4096]{1,0:T(8,128)(2,1)S(1)} %bitcast.172, bf16[512,4096]{1,0:T(8,128)(2,1)} %collective-permute-done.1), kind=kOutput, calls=%fused_computation.201 | convolution fusion | flops 536936320 | bytes 5505536 | tf_op jit(solution)/shard_map/dot_general | solution.py:71
  137.7 3.8 %fusion.48 = (f32[128]{0:T(128)S(1)}, f32[128,512]{1,0:T(8,128)S(1)}) fusion(bf16[128,4096]{1,0:T(8,128)(2,1)S(1)} %bitcast.182, bf16[512,4096]{1,0:T(8,128)(2,1)} %collective-permute-done.1), kind=kOutput, calls=%fused_computation.199 | convolution fusion | flops 536936320 | bytes 5505536 | tf_op jit(solution)/shard_map/dot_general | solution.py:71
  141.9 4.1 %fusion.46 = (f32[128]{0:T(128)S(1)}, f32[128,512]{1,0:T(8,128)S(1)}) fusion(bf16[128,4096]{1,0:T(8,128)(2,1)} %bitcast.8, bf16[512,4096]{1,0:T(8,128)(2,1)} %collective-permute-done.1), kind=kOutput, calls=%fused_computation.197 | convolution fusion | flops 536936320 | bytes 5505536 | tf_op jit(solution)/shard_map/dot_general | solution.py:71
  146.4 4.1 %fusion.44 = (f32[128]{0:T(128)S(1)}, f32[128,512]{1,0:T(8,128)S(1)}) fusion(bf16[128,4096]{1,0:T(8,128)(2,1)} %bitcast.1, bf16[512,4096]{1,0:T(8,128)(2,1)} %collective-permute-done.1), kind=kOutput, calls=%fused_computation.195 | convolution fusion | flops 536936320 | bytes 5505536 | tf_op jit(solution)/shard_map/dot_general | solution.py:71
  151.0 3.8 %fusion.42 = (f32[128]{0:T(128)S(1)}, f32[128,512]{1,0:T(8,128)S(1)}) fusion(bf16[128,4096]{1,0:T(8,128)(2,1)S(1)} %bitcast.174, bf16[512,4096]{1,0:T(8,128)(2,1)} %collective-permute-done.1), kind=kOutput, calls=%fused_computation.193 | convolution fusion | flops 536936320 | bytes 5505536 | tf_op jit(solution)/shard_map/dot_general | solution.py:71
  155.3 4.0 %fusion.40 = (f32[128]{0:T(128)S(1)}, f32[128,512]{1,0:T(8,128)S(1)}) fusion(bf16[128,4096]{1,0:T(8,128)(2,1)S(1)} %bitcast.180, bf16[512,4096]{1,0:T(8,128)(2,1)} %collective-permute-done.1), kind=kOutput, calls=%fused_computation.191 | convolution fusion | flops 536936320 | bytes 5505536 | tf_op jit(solution)/shard_map/dot_general | solution.py:71
  159.7 3.8 %fusion.38 = (f32[128]{0:T(128)S(1)}, f32[128,512]{1,0:T(8,128)S(1)}) fusion(bf16[128,4096]{1,0:T(8,128)(2,1)S(1)} %bitcast.178, bf16[512,4096]{1,0:T(8,128)(2,1)} %collective-permute-done.1), kind=kOutput, calls=%fused_computation.189 | convolution fusion | flops 536936320 | bytes 5505536 | tf_op jit(solution)/shard_map/dot_general | solution.py:71
  163.8 3.8 %fusion.36 = (f32[128]{0:T(128)S(1)}, f32[128,512]{1,0:T(8,128)S(1)}) fusion(bf16[128,4096]{1,0:T(8,128)(2,1)S(1)} %bitcast.176, bf16[512,4096]{1,0:T(8,128)(2,1)} %collective-permute-done.1), kind=kOutput, calls=%fused_computation.187 | convolution fusion | flops 536936320 | bytes 5505536 | tf_op jit(solution)/shard_map/dot_general | solution.py:71
  168.5 15.1 %all_to_all.26 = f32[8,2,128]{2,1,0:T(2,128)S(1)} all-to-all(f32[8,2,128]{2,1,0:T(2,128)S(1)} %reshape.1002), channel_id=1, replica_groups=mesh['z'=8,'c'=2,'y'=4,'x'=4] {'z'}, dimensions={0} | all-to-all | bytes 16384 | tf_op jit(solution)/shard_map/all_to_all | solution.py:96
  184.2 15.2 %all-to-all-start.4 = ((f32[16,2,128]{2,1,0:T(2,128)}), f32[16,2,128]{2,1,0:T(2,128)S(1)}, u32[]{:S(2)}, u32[]{:S(2)}) async-start(f32[16,2,128]{2,1,0:T(2,128)} %broadcast_in_dim.61), calls=%async_computation.4 | async-start | bytes 32768 | tf_op jit(solution)/shard_map/all_to_all | solution.py:15
  200.1 5.6 %all-to-all-done.4 = f32[16,2,128]{2,1,0:T(2,128)S(1)} async-done(((f32[16,2,128]{2,1,0:T(2,128)}), f32[16,2,128]{2,1,0:T(2,128)S(1)}, u32[]{:S(2)}, u32[]{:S(2)}) %all-to-all-start.4) | async-done | bytes 16416 | tf_op jit(solution)/shard_map/all_to_all | solution.py:15
  206.7 1.3 exponential_reduce_fusion.18
  (145 shorter events, 15.1 us)
Async XLA Ops:
  31.7 17.8 %all-to-all-start.1 = ((bf16[4,4,8,4096]{3,2,1,0:T(8,128)(2,1)}), bf16[4,4,8,4096]{3,2,1,0:T(8,128)(2,1)S(1)}, u32[]{:S(2)}, u32[]{:S(2)}) async-start(bf16[4,4,8,4096]{3,2,1,0:T(8,128)(2,1)} %broadcast_in_dim.58), calls=%async_computation.1 | async-start | bytes 2097152 | tf_op jit(solution)/shard_map/all_to_all | solution.py:15
  36.2 97.3 %collective-permute-start.1 = (bf16[512,4096]{1,0:T(8,128)(2,1)}, bf16[512,4096]{1,0:T(8,128)(2,1)}, u32[]{:S(2)}, u32[]{:S(2)}) collective-permute-start(bf16[512,4096]{1,0:T(8,128)(2,1)} %param.13), channel_id=1, source_target_pairs={{0,16},{16,0},{1,17},{17,1},{2,18},{18,2},{3,19},{19,3},{4,20},{20... | collective-permute-start | bytes 12582920 | tf_op jit(solution)/shard_map/ppermute | solution.py:22
  50.6 38.8 %all-to-all-start.2 = ((bf16[4,4,8,4096]{3,2,1,0:T(8,128)(2,1)}), bf16[4,4,8,4096]{3,2,1,0:T(8,128)(2,1)S(1)}, u32[]{:S(2)}, u32[]{:S(2)}) async-start(bf16[4,4,8,4096]{3,2,1,0:T(8,128)(2,1)} %broadcast_in_dim.60), calls=%async_computation.2 | async-start | bytes 2097152 | tf_op jit(solution)/shard_map/all_to_all | solution.py:15
  55.5 40.8 %collective-permute-start.3 = (bf16[4,4,8,4096]{3,2,1,0:T(8,128)(2,1)S(1)}, bf16[4,4,8,4096]{3,2,1,0:T(8,128)(2,1)S(1)}, u32[]{:S(2)}, u32[]{:S(2)}) collective-permute-start(bf16[4,4,8,4096]{3,2,1,0:T(8,128)(2,1)S(1)} %all-to-all-done.1), channel_id=1, source_target_pairs={{0,1},{1,2},{2,3},{3,0},{4,5},{5,6},{6,7},{7,4},{8,9},{9,10},{10,1... | collective-permute-start | bytes 3145736 | tf_op jit(solution)/shard_map/ppermute | solution.py:22
  58.7 41.0 %collective-permute-start.2 = (bf16[4,4,8,4096]{3,2,1,0:T(8,128)(2,1)S(1)}, bf16[4,4,8,4096]{3,2,1,0:T(8,128)(2,1)}, u32[]{:S(2)}, u32[]{:S(2)}) collective-permute-start(bf16[4,4,8,4096]{3,2,1,0:T(8,128)(2,1)S(1)} %all-to-all-done.1), channel_id=1, source_target_pairs={{0,2},{1,3},{2,0},{3,1},{4,6},{5,7},{6,4},{7,5},{8,10},{9,11},{10,... | collective-permute-start | bytes 3145736 | tf_op jit(solution)/shard_map/ppermute | solution.py:22
  59.4 51.4 %collective-permute-start = (bf16[4,4,8,4096]{3,2,1,0:T(8,128)(2,1)S(1)}, bf16[4,4,8,4096]{3,2,1,0:T(8,128)(2,1)}, u32[]{:S(2)}, u32[]{:S(2)}) collective-permute-start(bf16[4,4,8,4096]{3,2,1,0:T(8,128)(2,1)S(1)} %all-to-all-done.1), channel_id=1, source_target_pairs={{0,3},{1,0},{2,1},{3,2},{4,7},{5,4},{6,5},{7,6},{8,11},{9,8},{10,9... | collective-permute-start | bytes 3145736 | tf_op jit(solution)/shard_map/ppermute | solution.py:22
  89.4 4.6 %copy-start = (bf16[512,4096]{1,0:T(8,128)(2,1)S(1)}, bf16[512,4096]{1,0:T(8,128)(2,1)}, u32[]{:S(2)}) copy-start(bf16[512,4096]{1,0:T(8,128)(2,1)} %param.13) | copy-start | bytes 12582916
  89.5 32.9 %collective-permute-start.6 = (bf16[4,4,8,4096]{3,2,1,0:T(8,128)(2,1)S(1)}, bf16[4,4,8,4096]{3,2,1,0:T(8,128)(2,1)S(1)}, u32[]{:S(2)}, u32[]{:S(2)}) collective-permute-start(bf16[4,4,8,4096]{3,2,1,0:T(8,128)(2,1)S(1)} %all-to-all-done.2), channel_id=1, source_target_pairs={{0,4},{4,8},{8,12},{12,0},{1,5},{5,9},{9,13},{13,1},{2,6},{6,10},{... | collective-permute-start | bytes 3145736 | tf_op jit(solution)/shard_map/ppermute | solution.py:22
  96.3 3.4 %copy-start.5 = (bf16[4,4,8,4096]{3,2,1,0:T(8,128)(2,1)}, bf16[4,4,8,4096]{3,2,1,0:T(8,128)(2,1)S(1)}, u32[]{:S(2)}) copy-start(bf16[4,4,8,4096]{3,2,1,0:T(8,128)(2,1)S(1)} %collective-permute-done.3) | copy-start | bytes 3145732
  96.3 28.3 %collective-permute-start.5 = (bf16[4,4,8,4096]{3,2,1,0:T(8,128)(2,1)S(1)}, bf16[4,4,8,4096]{3,2,1,0:T(8,128)(2,1)S(1)}, u32[]{:S(2)}, u32[]{:S(2)}) collective-permute-start(bf16[4,4,8,4096]{3,2,1,0:T(8,128)(2,1)S(1)} %all-to-all-done.2), channel_id=1, source_target_pairs={{0,8},{4,12},{8,0},{12,4},{1,9},{5,13},{9,1},{13,5},{2,10},{6,14},... | collective-permute-start | bytes 3145736 | tf_op jit(solution)/shard_map/ppermute | solution.py:22
  99.8 32.1 %collective-permute-start.4 = (bf16[4,4,8,4096]{3,2,1,0:T(8,128)(2,1)S(1)}, bf16[4,4,8,4096]{3,2,1,0:T(8,128)(2,1)S(1)}, u32[]{:S(2)}, u32[]{:S(2)}) collective-permute-start(bf16[4,4,8,4096]{3,2,1,0:T(8,128)(2,1)S(1)} %all-to-all-done.2), channel_id=1, source_target_pairs={{0,12},{4,0},{8,4},{12,8},{1,13},{5,1},{9,5},{13,9},{2,14},{6,2},{... | collective-permute-start | bytes 3145736 | tf_op jit(solution)/shard_map/ppermute | solution.py:22
  122.4 4.5 %copy-start.3 = (bf16[4,4,8,4096]{3,2,1,0:T(8,128)(2,1)}, bf16[4,4,8,4096]{3,2,1,0:T(8,128)(2,1)S(1)}, u32[]{:S(2)}) copy-start(bf16[4,4,8,4096]{3,2,1,0:T(8,128)(2,1)S(1)} %collective-permute-done.6) | copy-start | bytes 3145732
  124.6 8.9 %copy-start.1 = (bf16[4,4,8,4096]{3,2,1,0:T(8,128)(2,1)}, bf16[4,4,8,4096]{3,2,1,0:T(8,128)(2,1)S(1)}, u32[]{:S(2)}) copy-start(bf16[4,4,8,4096]{3,2,1,0:T(8,128)(2,1)S(1)} %collective-permute-done.5) | copy-start | bytes 3145732
  133.5 4.2 %copy-start.6 = (bf16[4,4,8,4096]{3,2,1,0:T(8,128)(2,1)S(1)}, bf16[4,4,8,4096]{3,2,1,0:T(8,128)(2,1)}, u32[]{:S(2)}) copy-start(bf16[4,4,8,4096]{3,2,1,0:T(8,128)(2,1)} %copy-done.5) | copy-start | bytes 3145732
  150.5 4.8 %copy-start.4 = (bf16[4,4,8,4096]{3,2,1,0:T(8,128)(2,1)S(1)}, bf16[4,4,8,4096]{3,2,1,0:T(8,128)(2,1)}, u32[]{:S(2)}) copy-start(bf16[4,4,8,4096]{3,2,1,0:T(8,128)(2,1)} %copy-done.3) | copy-start | bytes 3145732
  151.0 3.9 %copy-start.8 = (f32[128,512]{1,0:T(8,128)S(1)}, f32[128,512]{1,0:T(8,128)}, u32[]{:S(2)}) copy-start(f32[128,512]{1,0:T(8,128)} %get-tuple-element.122) | copy-start | bytes 786436
  154.9 4.5 %copy-start.9 = (f32[128,512]{1,0:T(8,128)S(1)}, f32[128,512]{1,0:T(8,128)}, u32[]{:S(2)}) copy-start(f32[128,512]{1,0:T(8,128)} %get-tuple-element.118) | copy-start | bytes 786436
  154.9 4.8 %copy-start.2 = (bf16[4,4,8,4096]{3,2,1,0:T(8,128)(2,1)S(1)}, bf16[4,4,8,4096]{3,2,1,0:T(8,128)(2,1)}, u32[]{:S(2)}) copy-start(bf16[4,4,8,4096]{3,2,1,0:T(8,128)(2,1)} %copy-done.1) | copy-start | bytes 3145732
  159.3 4.2 %copy-start.7 = (f32[128,512]{1,0:T(8,128)S(1)}, f32[128,512]{1,0:T(8,128)}, u32[]{:S(2)}) copy-start(f32[128,512]{1,0:T(8,128)} %get-tuple-element.114) | copy-start | bytes 786436
  184.2 21.5 %all-to-all-start.4 = ((f32[16,2,128]{2,1,0:T(2,128)}), f32[16,2,128]{2,1,0:T(2,128)S(1)}, u32[]{:S(2)}, u32[]{:S(2)}) async-start(f32[16,2,128]{2,1,0:T(2,128)} %broadcast_in_dim.61), calls=%async_computation.4 | async-start | bytes 32768 | tf_op jit(solution)/shard_map/all_to_all | solution.py:15
